TPU v7x, 128 devices: a whole 4x4x4 slice. The times are simulated.
128 devices in a mesh: row: 8 (over z, x_hi), col: 16 (over x_lo, y, core).
Axes of the slice: x: 4 (x_hi: 2, x_lo: 2; x = x_hi * 2 + x_lo), y: 4, z: 4, core: 2. Of those that a mesh axis runs over, the one named last changes fastest.
Arguments:
- eigvecs: bfloat16 [81920, 4096], P('row', 'col'), may hold values from -0.09375 to 0.09375
- reflectors: bfloat16 [2, 81920, 128], P(None, 'row'), may hold values from -6 to 6
- factors: float32 [2, 128, 128], replicated, may hold values from -0.00015258789 to 0.00015258789
- frequencies: float32 [4096], replicated, may hold values from 0.3 to 3
- region_blocks: int32 [72], P('row'), may hold values from 0 to 639, as said below
Outputs:
- covariance: float32 [9216, 9216], P('row', 'col')
Inputs may be any that keep to these rules, and one draw needn't show every extreme that they name: `region_blocks`: the 72 block numbers are distinct and ascending; exactly 9 of them lie in each consecutive run of 80 block numbers.
All inputs are finite; a program needn't handle non-finite values.
Results may differ from a plain program's by a relative error of at most 0.004.
Values may be sent and summed in bfloat16 or wider, within the bound.
No kernel may reach another device: no remote copies, remote signals or barrier semaphores. Data moves between devices by JAX's collectives and lax.ppermute only.
A program may use at most 128 MiB of HBM per device.

v0:
```python
import jax
import jax.numpy as jnp
from jax import lax
from jax.sharding import PartitionSpec as P

BLOCK = 128


def from_everyone(shard, axis):
    copies = jnp.broadcast_to(shard, (lax.axis_size(axis), *shard.shape))
    return lax.all_to_all(copies, axis, split_axis=0, concat_axis=0, tiled=True)


def over_copies(shard, axis):
    everything = from_everyone(shard, axis)
    return jnp.sum(everything, axis=0)


def contract_rows(left, right):
    return lax.dot_general(
        left, right, (((0,), (0,)), ((), ())), preferred_element_type=jnp.float32
    )


def contract_cols(left, right):
    return lax.dot_general(
        left, right, (((1,), (1,)), ((), ())), preferred_element_type=jnp.float32
    )


def per_device(eigvecs, reflectors, factors, frequencies, region_blocks):
    highest = lax.Precision.HIGHEST
    first_block = reflectors[0]
    second_block = reflectors[1]
    first_factor = jnp.triu(factors[0])
    second_factor = jnp.triu(factors[1])
    second_local = contract_rows(second_block, eigvecs)
    second_proj = over_copies(second_local, "row")
    second_apply = jnp.dot(second_factor, second_proj, precision=highest).astype(jnp.bfloat16)
    cross_local = contract_rows(first_block, second_block)
    first_local = contract_rows(first_block, eigvecs) - jnp.dot(
        cross_local, second_apply.astype(jnp.float32), precision=highest
    )
    first_proj = over_copies(first_local, "row")
    first_apply = jnp.dot(first_factor, first_proj, precision=highest).astype(jnp.bfloat16)
    local_blocks = eigvecs.shape[0] // BLOCK
    columns = eigvecs.shape[1]
    width = reflectors.shape[2]
    local_index = region_blocks - lax.axis_index("row") * local_blocks
    picked_vecs = jnp.take(
        eigvecs.reshape(local_blocks, BLOCK, columns), local_index, axis=0
    ).reshape(-1, columns)
    picked_refl = jnp.take(
        reflectors.reshape(2, local_blocks, BLOCK, width), local_index, axis=1
    ).reshape(2, -1, width)
    region = picked_vecs.astype(jnp.float32)
    region = region - jnp.dot(picked_refl[1], second_apply, preferred_element_type=jnp.float32)
    region = region - jnp.dot(picked_refl[0], first_apply, preferred_element_type=jnp.float32)
    region = region.astype(jnp.bfloat16)
    weight_all = 1.0 / jnp.tanh(frequencies / 2.0) / (2.0 * frequencies)
    column_index = lax.axis_index("col")
    weight = lax.dynamic_slice_in_dim(weight_all, column_index * columns, columns, 0)
    scaled = (region.astype(jnp.float32) * weight[None, :]).astype(jnp.bfloat16)
    whole = lax.all_gather(region, "row", axis=0, tiled=True)
    partner = lax.all_to_all(whole, "col", split_axis=0, concat_axis=1, tiled=True)
    return contract_cols(lax.all_gather(scaled, "col", axis=1, tiled=True), partner)


def solution(mesh):
    return jax.shard_map(
        per_device,
        mesh=mesh,
        in_specs=(P("row", "col"), P(None, "row", None), P(), P(), P("row")),
        out_specs=P("row", "col"),
        check_vma=False,
    )
```

profile of v0, /device:TPU:1, one launch (start us, length us, event | category | flops | bytes accessed | tf_op | source)
XLA Modules:
  0.0 266.3 jit_solution(2419679412700755586)
XLA Ops:
  6.5 4.3 %fusion.5 = f32[128,256]{1,0:T(8,128)S(1)} fusion(bf16[10240,256]{1,0:T(8,128)(2,1)} %param.5, bf16[2,10240,128]{2,1,0:T(8,128)(2,1)} %param.6), kind=kOutput, calls=%fused_computation.9 | convolution fusion | flops 671088640 | bytes 7995392 | tf_op jit(solution)/shard_map/dot_general | solution.py:20
  10.9 1.1 broadcast_in_dim.46
  11.9 8.3 %all-to-all-start = ((f32[8,128,256]{2,1,0:T(8,128)}), f32[8,128,256]{2,1,0:T(8,128)S(1)}, u32[]{:S(2)}, u32[]{:S(2)}) async-start(f32[8,128,256]{2,1,0:T(8,128)} %broadcast_in_dim.46), calls=%async_computation | async-start | bytes 2097152 | tf_op jit(solution)/shard_map/all_to_all | solution.py:11
  20.3 3.1 %gather_fusion.1 = bf16[9,2,128,128]{3,2,1,0:T(8,128)(2,1)S(1)} fusion(bf16[2,80,128,128]{3,2,1,0:T(8,128)(2,1)} %bitcast.46, s32[1024]{0:T(1024)S(1)} %pad_clamp_fusion), kind=kCustom, calls=%fused_computation.1 | custom fusion | bytes 1179684 | tf_op jit(solution)/shard_map/jit(_take)/gather | solution.py:53
  23.6 3.6 %fusion = f32[128,128]{1,0:T(8,128)S(1)} fusion(bf16[2,10240,128]{2,1,0:T(8,128)(2,1)} %param.6), kind=kOutput, calls=%fused_computation.4 | convolution fusion | flops 335544320 | bytes 5308416 | tf_op jit(solution)/shard_map/dot_general | solution.py:20
  27.3 2.8 %fusion.2 = f32[128,256]{1,0:T(8,128)S(1)} fusion(bf16[10240,256]{1,0:T(8,128)(2,1)S(1)} %bitcast.44, bf16[2,10240,128]{2,1,0:T(8,128)(2,1)} %param.6), kind=kOutput, calls=%fused_computation.6 | convolution fusion | flops 671088640 | bytes 7995392 | tf_op jit(solution)/shard_map/dot_general | solution.py:20
  30.2 6.1 %all-to-all-done = f32[8,128,256]{2,1,0:T(8,128)S(1)} async-done(((f32[8,128,256]{2,1,0:T(8,128)}), f32[8,128,256]{2,1,0:T(8,128)S(1)}, u32[]{:S(2)}, u32[]{:S(2)}) %all-to-all-start) | async-done | bytes 1048608 | tf_op jit(solution)/shard_map/all_to_all | solution.py:11
  36.3 0.3 convolution_convert_fusion.1
  36.6 0.2 convolution_subtract_fusion.2
  36.9 1.1 broadcast_in_dim.47
  37.9 4.1 %all-to-all-start.1 = ((f32[8,128,256]{2,1,0:T(8,128)}), f32[8,128,256]{2,1,0:T(8,128)S(1)}, u32[]{:S(2)}, u32[]{:S(2)}) async-start(f32[8,128,256]{2,1,0:T(8,128)} %broadcast_in_dim.47), calls=%async_computation.1 | async-start | bytes 2097152 | tf_op jit(solution)/shard_map/all_to_all | solution.py:11
  42.2 3.1 %gather_fusion = bf16[9,128,256]{2,1,0:T(8,128)(2,1)S(1)} fusion(bf16[80,128,256]{2,1,0:T(8,128)(2,1)} %bitcast.42, s32[1024]{0:T(1024)S(1)} %pad_clamp_fusion), kind=kCustom, calls=%fused_computation | custom fusion | bytes 1179684 | tf_op jit(solution)/shard_map/jit(_take)/gather | solution.py:50
  45.2 0.8 multiply_divide_fusion
  46.0 0.2 bitcast_select_fusion
  46.2 0.3 convolution_subtract_fusion.1
  46.5 10.9 %all-to-all-done.1 = f32[8,128,256]{2,1,0:T(8,128)S(1)} async-done(((f32[8,128,256]{2,1,0:T(8,128)}), f32[8,128,256]{2,1,0:T(8,128)S(1)}, u32[]{:S(2)}, u32[]{:S(2)}) %all-to-all-start.1) | async-done | bytes 1048608 | tf_op jit(solution)/shard_map/all_to_all | solution.py:11
  57.5 0.3 convolution_convert_fusion
  57.8 1.3 multiply_convert_fusion
  59.2 0.7 all-gather.3.cloned.1.call-update
  59.9 74.4 %all-gather.5.cloned.1.call-done = bf16[9216,256]{1,0:T(8,128)(2,1)} async-done(((bf16[1152,256]{1,0:T(8,128)(2,1)}), bf16[9216,256]{1,0:T(8,128)(2,1)}) %all-gather.5.cloned.1.call-update) | async-done | bytes 4718608 | tf_op jit(solution)/shard_map/all_gather | solution.py:64
  134.3 77.2 %all_to_all.29 = bf16[16,576,256]{2,1,0:T(8,128)(2,1)S(1)} all-to-all(bf16[16,576,256]{2,1,0:T(8,128)(2,1)} %bitcast.47), channel_id=1, replica_groups=mesh['row'=8,'col'=16] {'col'}, dimensions={0} | all-to-all | bytes 9437184 | tf_op jit(solution)/shard_map/all_to_all | solution.py:65
  211.5 2.9 %copy.9 = bf16[16,72,8,256]{3,2,0,1:T(8,128)(2,1)} copy(bf16[16,72,8,256]{3,2,1,0:T(8,128)(2,1)S(1)} %bitcast.45) | data formatting | bytes 9437184 | tf_op jit(solution)/shard_map/all_to_all | solution.py:65
  214.4 33.2 %all-gather.3.cloned.1.call-done = bf16[1152,4096]{1,0:T(8,128)(2,1)} async-done(((bf16[1152,256]{1,0:T(8,128)(2,1)}), bf16[1152,4096]{1,0:T(8,128)(2,1)}) %all-gather.3.cloned.1.call-update) | async-done | bytes 9437200 | tf_op jit(solution)/shard_map/all_gather | solution.py:66
  247.5 12.0 %fusion.21 = f32[1152,576]{0,1:T(8,128)} fusion(bf16[1152,4096]{1,0:T(8,128)(2,1)} %all-gather.3.cloned.1.call-done, bf16[576,4096]{1,0:T(8,128)(2,1)} %bitcast.48), kind=kOutput, calls=%fused_computation.40 | convolution fusion | flops 5435817984 | bytes 16809984 | tf_op jit(solution)/shard_map/dot_general | solution.py:26
  (20 shorter events, 0.6 us)
Async XLA Ops:
  6.5 13.7 %copy-start.1 = (s32[9]{0:T(128)S(1)}, s32[9]{0:T(128)}, u32[]{:S(2)}) copy-start(s32[9]{0:T(128)} %param.9) | copy-start | bytes 112
  10.9 16.4 %slice-start = ((s8[5242880]{0:T(1024)(128)(4,1)}), s8[1048576]{0:T(1024)(128)(4,1)S(1)}, s32[]{:S(2)}) async-start(s8[5242880]{0:T(1024)(128)(4,1)} %bitcast.43), calls=%async_computation.5 | async-start | bytes 2097152
  11.9 24.3 %all-to-all-start = ((f32[8,128,256]{2,1,0:T(8,128)}), f32[8,128,256]{2,1,0:T(8,128)S(1)}, u32[]{:S(2)}, u32[]{:S(2)}) async-start(f32[8,128,256]{2,1,0:T(8,128)} %broadcast_in_dim.46), calls=%async_computation | async-start | bytes 2097152 | tf_op jit(solution)/shard_map/all_to_all | solution.py:11
  23.6 3.8 %slice-start.1 = ((s8[5242880]{0:T(1024)(128)(4,1)}), s8[4194304]{0:T(1024)(128)(4,1)S(1)}, s32[]{:S(2)}) async-start(s8[5242880]{0:T(1024)(128)(4,1)} %bitcast.43), calls=%async_computation.6 | async-start | bytes 8388608
  27.3 9.0 %copy-start = (f32[2,128,128]{2,1,0:T(8,128)S(1)}, f32[2,128,128]{2,1,0:T(8,128)}, u32[]{:S(2)}) copy-start(f32[2,128,128]{2,1,0:T(8,128)} %param.7) | copy-start | bytes 393220
  37.9 19.5 %all-to-all-start.1 = ((f32[8,128,256]{2,1,0:T(8,128)}), f32[8,128,256]{2,1,0:T(8,128)S(1)}, u32[]{:S(2)}, u32[]{:S(2)}) async-start(f32[8,128,256]{2,1,0:T(8,128)} %broadcast_in_dim.47), calls=%async_computation.1 | async-start | bytes 2097152 | tf_op jit(solution)/shard_map/all_to_all | solution.py:11
  42.0 92.3 %all-gather.5.cloned.1.call-start = ((), (), s32[]{:S(2)}) async-start(), calls=%async_computation.4 | async-start | bytes 5308416 | tf_op jit(solution)/shard_map/all_gather | solution.py:64
  59.2 188.4 %all-gather.3.cloned.1.call-start = ((), (), s32[]{:S(2)}) async-start(), calls=%async_computation.3 | async-start | bytes 10027008 | tf_op jit(solution)/shard_map/all_gather | solution.py:66
Sparse Core Ops, SparseCore 0:
  59.3 74.9 all-gather.4
  135.9 111.5 all-gather.2
where the time goes:
time: 267 us; the launch traced here: 266 us
  waiting for transfers between devices  125 us (47%)
  blocking collectives  77.2 us (29%)
  matrix products  25.1 us (9%)
  between operations  13.6 us (5%)
  starting transfers between devices  12.5 us (5%)
  local copies, waits for them, and re-layouts  11.4 us (4%)
    all_to_all x1, blocking collectives, per_device(): lax.all_to_all(whole, 'col', split_axis=0, concat_axis=1, tiled=True)  77.2 us
    all_gather x1, waiting for transfers between devices, per_device(): whole = lax.all_gather(region, 'row', axis=0, tiled=True)  74.4 us
    all_gather x1, waiting for transfers between devices, per_device(): lax.all_gather(scaled, 'col', axis=1, tiled=True)  33.2 us
    all_to_all x2, waiting for transfers between devices, from_everyone(): return lax.all_to_all(copies, axis, split_axis=0, concat_axis=0, tiled=True)  17 us
    all_to_all x2, starting transfers between devices, from_everyone(): return lax.all_to_all(copies, axis, split_axis=0, concat_axis=0, tiled=True)  12.4 us
    dot_general x1, matrix products, contract_cols(): lax.dot_general(left, right, (((1,), (1,)), ((), ())), preferred_element_...  12 us
    dot_general x3, matrix products, contract_rows(): lax.dot_general(left, right, (((0,), (0,)), ((), ())), preferred_element_...  10.7 us
  transfers between devices with their start and end apart: 4, of which 4 were waited for; matrix products, arithmetic and copies ran while one was open for 6% of the time, Pallas kernels for 0%

commit v1 on v0

--- a/solution.py
+++ b/solution.py
@@ -63,7 +63,12 @@
     scaled = (region.astype(jnp.float32) * weight[None, :]).astype(jnp.bfloat16)
     whole = lax.all_gather(region, "row", axis=0, tiled=True)
     partner = lax.all_to_all(whole, "col", split_axis=0, concat_axis=1, tiled=True)
-    return contract_cols(lax.all_gather(scaled, "col", axis=1, tiled=True), partner)
+    return contract_cols(
+        jnp.concatenate(
+            lax.all_to_all(jnp.stack([scaled] * lax.axis_size("col")), "col", 0, 0), axis=1
+        ),
+        partner,
+    )
 
 
 def solution(mesh):

time: 267 us -> 306 us (1.15)
  waiting for transfers between devices: 125 us -> 166 us
  blocking collectives: 77.2 us -> 68.4 us
  starting transfers between devices: 12.5 us -> 19.8 us
    all_to_all x0 -> x1, waiting for transfers between devices: none -> 40.7 us  [per_device(): lax.all_to_all(jnp.stack([scaled] * lax.axis_size('col')), 'col', 0, 0)]
    all_gather x1, waiting for transfers between devices: 74.4 us -> 108 us  [per_device(): whole = lax.all_gather(region, 'row', axis=0, tiled=True)]
    all_gather x1 -> x0, waiting for transfers between devices: 33.2 us -> none  [per_device(): lax.all_gather(scaled, 'col', axis=1, tiled=True)]
    all_to_all x1, blocking collectives: 77.2 us -> 68.4 us  [per_device(): lax.all_to_all(whole, 'col', split_axis=0, concat_axis=1, tiled=True)]
    all_to_all x0 -> x1, starting transfers between devices: none -> 7.28 us  [per_device(): lax.all_to_all(jnp.stack([scaled] * lax.axis_size('col')), 'col', 0, 0)]
    another operation x0 -> x1, local copies, waits for them, and re-layouts: none -> 4.56 us  [per_device(): jnp.stack([scaled] * lax.axis_size('col'))]
  transfers between devices with their start and end apart: 4 -> 4, of which waited for: 4 -> 4; matrix products, arithmetic and copies ran while one was open for 6% -> 5% of each run, Pallas kernels for 0% -> 0%
where the time goes in v1:
time: 306 us
  waiting for transfers between devices  166 us (54%)
  blocking collectives  68.4 us (22%)
  matrix products  23.3 us (8%)
  starting transfers between devices  19.8 us (6%)
  between operations  13.6 us (4%)
  local copies, waits for them, and re-layouts  13.1 us (4%)
    all_gather x1, waiting for transfers between devices, per_device(): whole = lax.all_gather(region, 'row', axis=0, tiled=True)  108 us
    all_to_all x1, blocking collectives, per_device(): lax.all_to_all(whole, 'col', split_axis=0, concat_axis=1, tiled=True)  68.4 us
    all_to_all x1, waiting for transfers between devices, per_device(): lax.all_to_all(jnp.stack([scaled] * lax.axis_size('col')), 'col', 0, 0)  40.7 us
    all_to_all x2, waiting for transfers between devices, from_everyone(): return lax.all_to_all(copies, axis, split_axis=0, concat_axis=0, tiled=True)  17 us
    all_to_all x2, starting transfers between devices, from_everyone(): return lax.all_to_all(copies, axis, split_axis=0, concat_axis=0, tiled=True)  12.4 us
    dot_general x3, matrix products, contract_rows(): lax.dot_general(left, right, (((0,), (0,)), ((), ())), preferred_element_...  10.7 us
    dot_general x1, matrix products, contract_cols(): lax.dot_general(left, right, (((1,), (1,)), ((), ())), preferred_element_...  10.4 us
    all_to_all x1, starting transfers between devices, per_device(): lax.all_to_all(jnp.stack([scaled] * lax.axis_size('col')), 'col', 0, 0)  7.28 us
  transfers between devices with their start and end apart: 4, of which 4 were waited for; matrix products, arithmetic and copies ran while one was open for 5% of the time, Pallas kernels for 0%

profile of v1, /device:TPU:1, one launch (start us, length us, event | category | flops | bytes accessed | tf_op | source)
XLA Modules:
  0.0 305.8 jit_solution(5718852424751631668)
XLA Ops:
  6.5 4.3 %fusion.13 = f32[128,256]{1,0:T(8,128)S(1)} fusion(bf16[10240,256]{1,0:T(8,128)(2,1)} %param.5, bf16[2,10240,128]{2,1,0:T(8,128)(2,1)} %param.6), kind=kOutput, calls=%fused_computation.13 | convolution fusion | flops 671088640 | bytes 7995392 | tf_op jit(solution)/shard_map/dot_general | solution.py:20
  10.9 1.1 broadcast_in_dim.46
  11.9 8.3 %all-to-all-start = ((f32[8,128,256]{2,1,0:T(8,128)}), f32[8,128,256]{2,1,0:T(8,128)S(1)}, u32[]{:S(2)}, u32[]{:S(2)}) async-start(f32[8,128,256]{2,1,0:T(8,128)} %broadcast_in_dim.46), calls=%async_computation | async-start | bytes 2097152 | tf_op jit(solution)/shard_map/all_to_all | solution.py:11
  20.3 3.1 %gather_fusion.1 = bf16[9,2,128,128]{3,2,1,0:T(8,128)(2,1)S(1)} fusion(bf16[2,80,128,128]{3,2,1,0:T(8,128)(2,1)} %bitcast.52, s32[1024]{0:T(1024)S(1)} %pad_clamp_fusion), kind=kCustom, calls=%fused_computation.1 | custom fusion | bytes 1179684 | tf_op jit(solution)/shard_map/jit(_take)/gather | solution.py:53
  23.6 3.6 %fusion.8 = f32[128,128]{1,0:T(8,128)S(1)} fusion(bf16[2,10240,128]{2,1,0:T(8,128)(2,1)} %param.6), kind=kOutput, calls=%fused_computation.8 | convolution fusion | flops 335544320 | bytes 5308416 | tf_op jit(solution)/shard_map/dot_general | solution.py:20
  27.3 2.8 fusion.10
  30.2 6.1 %all-to-all-done = f32[8,128,256]{2,1,0:T(8,128)S(1)} async-done(((f32[8,128,256]{2,1,0:T(8,128)}), f32[8,128,256]{2,1,0:T(8,128)S(1)}, u32[]{:S(2)}, u32[]{:S(2)}) %all-to-all-start) | async-done | bytes 1048608 | tf_op jit(solution)/shard_map/all_to_all | solution.py:11
  36.3 0.3 convolution_convert_fusion.1
  36.9 1.1 broadcast_in_dim.47
  37.9 4.1 %all-to-all-start.1 = ((f32[8,128,256]{2,1,0:T(8,128)}), f32[8,128,256]{2,1,0:T(8,128)S(1)}, u32[]{:S(2)}, u32[]{:S(2)}) async-start(f32[8,128,256]{2,1,0:T(8,128)} %broadcast_in_dim.47), calls=%async_computation.1 | async-start | bytes 2097152 | tf_op jit(solution)/shard_map/all_to_all | solution.py:11
  42.1 3.1 %gather_fusion = bf16[9,128,256]{2,1,0:T(8,128)(2,1)S(1)} fusion(bf16[80,128,256]{2,1,0:T(8,128)(2,1)} %bitcast.49, s32[1024]{0:T(1024)S(1)} %pad_clamp_fusion), kind=kCustom, calls=%fused_computation | custom fusion | bytes 1179684 | tf_op jit(solution)/shard_map/jit(_take)/gather | solution.py:50
  45.2 0.8 multiply_divide_fusion
  46.0 0.2 bitcast_select_fusion
  46.2 0.3 convolution_subtract_fusion.1
  46.5 10.9 %all-to-all-done.1 = f32[8,128,256]{2,1,0:T(8,128)S(1)} async-done(((f32[8,128,256]{2,1,0:T(8,128)}), f32[8,128,256]{2,1,0:T(8,128)S(1)}, u32[]{:S(2)}, u32[]{:S(2)}) %all-to-all-start.1) | async-done | bytes 1048608 | tf_op jit(solution)/shard_map/all_to_all | solution.py:11
  57.5 0.3 convolution_convert_fusion
  57.8 1.1 multiply_convert_fusion
  59.0 4.6 %stack.2 = bf16[16,1152,256]{2,1,0:T(8,128)(2,1)} broadcast(bf16[1152,256]{1,0:T(8,128)(2,1)S(1)} %get-tuple-element.9), dimensions={1,2} | broadcast | bytes 10027008 | tf_op jit(solution)/shard_map/stack | solution.py:68
  63.5 7.3 %all-to-all-start.2 = ((bf16[16,1152,256]{2,1,0:T(8,128)(2,1)}), bf16[16,1152,256]{2,1,0:T(8,128)(2,1)}, u32[]{:S(2)}, u32[]{:S(2)}) async-start(bf16[16,1152,256]{2,1,0:T(8,128)(2,1)} %stack.2), calls=%async_computation.2 | async-start | bytes 18874368 | tf_op jit(solution)/shard_map/all_to_all | solution.py:68
  70.8 0.7 all-gather.2.cloned.1.call-update
  71.5 108.0 %all-gather.2.cloned.1.call-done = bf16[9216,256]{1,0:T(8,128)(2,1)} async-done(((bf16[1152,256]{1,0:T(8,128)(2,1)}), bf16[9216,256]{1,0:T(8,128)(2,1)}) %all-gather.2.cloned.1.call-update) | async-done | bytes 4718608 | tf_op jit(solution)/shard_map/all_gather | solution.py:64
  179.5 40.7 %all-to-all-done.2 = bf16[16,1152,256]{2,1,0:T(8,128)(2,1)} async-done(((bf16[16,1152,256]{2,1,0:T(8,128)(2,1)}), bf16[16,1152,256]{2,1,0:T(8,128)(2,1)}, u32[]{:S(2)}, u32[]{:S(2)}) %all-to-all-start.2) | async-done | bytes 9437216 | tf_op jit(solution)/shard_map/all_to_all | solution.py:68
  220.2 68.4 %all_to_all.31 = bf16[16,576,256]{2,1,0:T(8,128)(2,1)S(1)} all-to-all(bf16[16,576,256]{2,1,0:T(8,128)(2,1)} %bitcast.53), channel_id=1, replica_groups=mesh['row'=8,'col'=16] {'col'}, dimensions={0} | all-to-all | bytes 9437184 | tf_op jit(solution)/shard_map/all_to_all | solution.py:65
  288.5 10.4 %fusion.3 = f32[1152,576]{0,1:T(8,128)} fusion(bf16[16,576,256]{2,1,0:T(8,128)(2,1)S(1)} %all_to_all.31, bf16[16,1152,256]{2,1,0:T(8,128)(2,1)} %all-to-all-done.2), kind=kOutput, calls=%fused_computation.5 | convolution fusion | flops 5435817984 | bytes 16809984 | tf_op jit(solution)/shard_map/dot_general | solution.py:26
  (19 shorter events, 0.8 us)
Async XLA Ops:
  6.5 13.7 %copy-start.1 = (s32[9]{0:T(128)S(1)}, s32[9]{0:T(128)}, u32[]{:S(2)}) copy-start(s32[9]{0:T(128)} %param.9) | copy-start | bytes 112
  10.9 16.4 %slice-start = ((s8[5242880]{0:T(1024)(128)(4,1)}), s8[1048576]{0:T(1024)(128)(4,1)S(1)}, s32[]{:S(2)}) async-start(s8[5242880]{0:T(1024)(128)(4,1)} %bitcast.50), calls=%async_computation.5 | async-start | bytes 2097152
  11.9 24.3 %all-to-all-start = ((f32[8,128,256]{2,1,0:T(8,128)}), f32[8,128,256]{2,1,0:T(8,128)S(1)}, u32[]{:S(2)}, u32[]{:S(2)}) async-start(f32[8,128,256]{2,1,0:T(8,128)} %broadcast_in_dim.46), calls=%async_computation | async-start | bytes 2097152 | tf_op jit(solution)/shard_map/all_to_all | solution.py:11
  23.6 3.8 %slice-start.1 = ((s8[5242880]{0:T(1024)(128)(4,1)}), s8[4194304]{0:T(1024)(128)(4,1)S(1)}, s32[]{:S(2)}) async-start(s8[5242880]{0:T(1024)(128)(4,1)} %bitcast.50), calls=%async_computation.6 | async-start | bytes 8388608
  27.3 9.0 %copy-start = (f32[2,128,128]{2,1,0:T(8,128)S(1)}, f32[2,128,128]{2,1,0:T(8,128)}, u32[]{:S(2)}) copy-start(f32[2,128,128]{2,1,0:T(8,128)} %param.7) | copy-start | bytes 393220
  37.9 19.5 %all-to-all-start.1 = ((f32[8,128,256]{2,1,0:T(8,128)}), f32[8,128,256]{2,1,0:T(8,128)S(1)}, u32[]{:S(2)}, u32[]{:S(2)}) async-start(f32[8,128,256]{2,1,0:T(8,128)} %broadcast_in_dim.47), calls=%async_computation.1 | async-start | bytes 2097152 | tf_op jit(solution)/shard_map/all_to_all | solution.py:11
  63.5 156.6 %all-to-all-start.2 = ((bf16[16,1152,256]{2,1,0:T(8,128)(2,1)}), bf16[16,1152,256]{2,1,0:T(8,128)(2,1)}, u32[]{:S(2)}, u32[]{:S(2)}) async-start(bf16[16,1152,256]{2,1,0:T(8,128)(2,1)} %stack.2), calls=%async_computation.2 | async-start | bytes 18874368 | tf_op jit(solution)/shard_map/all_to_all | solution.py:68
  70.8 108.7 %all-gather.2.cloned.1.call-start = ((), (), s32[]{:S(2)}) async-start(), calls=%async_computation.4 | async-start | bytes 5308416 | tf_op jit(solution)/shard_map/all_gather | solution.py:64
Sparse Core Ops, SparseCore 0:
  73.9 105.5 all-gather.1
